TPU v7x, 256 devices: a whole 4x4x8 slice. The times are simulated.
256 devices in a mesh: sess: 32 (over y_hi, z, core), dp: 4 (over x), fsdp: 2 (over y_lo).
Axes of the slice: x: 4, y: 4 (y_hi: 2, y_lo: 2; y = y_hi * 2 + y_lo), z: 8, core: 2. Of those that a mesh axis runs over, the one named last changes fastest.
Arguments:
- unit_tokens: bfloat16 [4096, 128, 1024], P(('sess', 'dp', 'fsdp')), may hold values from -6 to 6
- block_owner: int32 [4096, 1], P(('sess', 'dp', 'fsdp')), may hold values from 0 to 31; in each aligned block of 16 rows (0 to 15, 16 to 31, ...) at most 2 rows name the same one
- block_clip: int32 [4096], P(('sess', 'dp', 'fsdp')), may hold values from 0 to 1
- block_valid: int32 [4096], P(('sess', 'dp', 'fsdp')), may hold values from 1 to 128, as said below
- latent_query_rows: bfloat16 [32, 1024], replicated, may hold values from -600 to 600
- latents: bfloat16 [32, 1024], replicated, may hold values from -1.5 to 1.5
- w_kv: bfloat16 [1024, 512], P('fsdp'), may hold values from -0.1875 to 0.1875
- w_out: bfloat16 [1024, 1024], P('fsdp'), may hold values from -0.75 to 0.75
- w_proj: bfloat16 [1024, 512], P('fsdp'), may hold values from -0.1875 to 0.1875
- movie_frame_embeddings: bfloat16 [512, 512], replicated, may hold values from -6 to 6
- clip_frame: int32 [512], P(('sess', 'dp', 'fsdp')), may hold values from 0 to 511
- logit_scale: float32 [1], replicated, may hold values from 40 to 60
Outputs:
- latent_state: bfloat16 [512, 32, 1024], P(('sess', 'dp', 'fsdp'))
- clip_loss: float32 [512], P(('sess', 'dp', 'fsdp'))
Inputs may be any that keep to these rules, and one draw needn't show every extreme that they name: `block_owner`: among the 16 blocks of one device no index is named more than 2 times, a bound that some block reaches. `block_valid`: the first block of every device is full.
All inputs are finite; a program needn't handle non-finite values.
Results may differ from a plain program's by a relative error of at most 0.009.
The roundings to bfloat16 on the way count: a program that leaves them out, or rounds other values in their place, can miss the bound.
Values may be sent and summed in bfloat16 or wider, within the bound.
A program may use at most 128 MiB of HBM per device.

v0:
```python
import math

import jax
import jax.numpy as jnp
from jax import lax
from jax.sharding import PartitionSpec as P

HEADS = 16
HEAD_DIM = 64
KV_HEADS = 4


def fold_rows(left, piece):
    return jnp.dot(left, piece, preferred_element_type=jnp.float32)


def keys_folded(left, weight):
    return fold_rows(left, lax.all_gather(weight, "fsdp", axis=0, tiled=True))


def output_folded(left, weight):
    return fold_rows(left, lax.all_gather(weight, "fsdp", axis=0, tiled=True))


def embed_folded(left, weight):
    return fold_rows(left, lax.all_gather(weight, "fsdp", axis=0, tiled=True))


def per_device(
    unit_tokens,
    block_owner,
    block_clip,
    block_valid,
    latent_query_rows,
    latents,
    w_kv,
    w_out,
    w_proj,
    movie_frame_embeddings,
    clip_frame,
    logit_scale,
):
    peers = lax.axis_size("sess")
    blocks_here, block_rows, width = unit_tokens.shape
    capacity = max(2, (2 * blocks_here + peers - 1) // peers)
    slots_all = peers * capacity
    kv_width = w_kv.shape[1] // 2
    group_size = HEADS // KV_HEADS
    clips_here = clip_frame.shape[0]
    lat_rows = latent_query_rows.shape[0]
    scaling = 1.0 / math.sqrt(HEAD_DIM)
    target = block_owner[:, 0]
    peer_hits = (target[:, None] == jnp.arange(peers, dtype=jnp.int32)[None, :]).astype(jnp.int32)
    preceding_value = jnp.cumsum(peer_hits, axis=0) - peer_hits
    rank_within = jnp.sum(preceding_value * peer_hits, axis=1)
    slot_of = target * capacity + rank_within
    placing = (slot_of[:, None] == jnp.arange(slots_all, dtype=jnp.int32)[None, :]).astype(
        jnp.bfloat16
    )
    meta_rows = jnp.stack([block_valid, block_clip], axis=1).astype(jnp.bfloat16)
    slot_meta = jnp.einsum("bs,bx->sx", placing, meta_rows, preferred_element_type=jnp.bfloat16)
    slot_meta = slot_meta.reshape(peers, capacity, 2)
    packed = jnp.einsum(
        "bs,bx->sx",
        placing,
        unit_tokens.reshape(blocks_here, block_rows * width),
        preferred_element_type=jnp.bfloat16,
    )
    packed = packed.reshape(peers, capacity, block_rows * width)
    arrived, arrived_meta = (
        lax.all_to_all(packed, "sess", split_axis=0, concat_axis=0, tiled=True),
        lax.all_to_all(slot_meta, "sess", split_axis=0, concat_axis=0, tiled=True),
    )
    kv_slots = keys_folded(arrived.reshape(slots_all * block_rows, width), w_kv).astype(
        jnp.bfloat16
    )
    kv_slots = kv_slots.reshape(slots_all, block_rows, 2 * kv_width)
    meta_float = arrived_meta.astype(jnp.float32).reshape(slots_all, 2)
    valid_count = meta_float[:, 0]
    slot_clip = meta_float[:, 1].astype(jnp.int32)
    row_live = jnp.arange(block_rows).astype(jnp.float32)[None, :] < valid_count[:, None]
    member = (slot_clip[None, :] == jnp.arange(clips_here, dtype=jnp.int32)[:, None]) & (
        valid_count[None, :] > 0.0
    )
    member_float = member.astype(jnp.float32)
    keys = kv_slots[:, :, :kv_width].reshape(slots_all, block_rows, KV_HEADS, HEAD_DIM)
    value_rows = kv_slots[:, :, kv_width:].reshape(slots_all, block_rows, KV_HEADS, HEAD_DIM)
    query = latent_query_rows.reshape(lat_rows, HEADS, HEAD_DIM)
    head_parts = []
    for head_position in range(HEADS):
        key_value_head = head_position // group_size
        scores = (
            jnp.einsum(
                "wa,pha->wph",
                query[:, head_position],
                keys[:, :, key_value_head],
                preferred_element_type=jnp.float32,
            )
            * scaling
        )
        scores = jnp.where(row_live[None], scores, -jnp.inf)
        slot_top = jnp.max(scores, axis=-1)
        clip_top = jnp.max(jnp.where(member[:, None, :], slot_top[None, :, :], -jnp.inf), axis=-1)
        clip_top = jnp.maximum(clip_top, 0.0)
        slot_shift = jnp.take(clip_top, slot_clip, axis=0)
        soft_terms = jnp.exp(scores - jnp.transpose(slot_shift)[..., None])
        slot_total = jnp.sum(soft_terms, axis=-1)
        clip_total = jnp.sum(slot_total[None, :, :] * member_float[:, None, :], axis=-1) + jnp.exp(
            -clip_top
        )
        rounded_result = soft_terms.astype(jnp.bfloat16)
        slot_sums = jnp.einsum(
            "ori,rin->orn",
            rounded_result,
            value_rows[:, :, key_value_head],
            preferred_element_type=jnp.float32,
        )
        clip_sums = jnp.einsum(
            "lsd,cs->cld", slot_sums, member_float, precision=lax.Precision.HIGHEST
        )
        head_parts.append(clip_sums / clip_total[..., None])
    attention = jnp.concatenate(head_parts, axis=-1).astype(jnp.bfloat16)
    mixed = output_folded(attention.reshape(clips_here * lat_rows, width), w_out)
    state = latents.astype(jnp.float32)[None] + mixed.reshape(clips_here, lat_rows, width)
    latent_state = state.astype(jnp.bfloat16)
    pooled = jnp.mean(state, axis=1).astype(jnp.bfloat16)
    embed = embed_folded(pooled, w_proj)
    embed_unit = (embed / jnp.sqrt(jnp.sum(embed * embed, axis=-1, keepdims=True) + 1e-06)).astype(
        jnp.bfloat16
    )
    frames = jnp.take(movie_frame_embeddings, clip_frame, axis=0).astype(jnp.float32)
    frame_unit = (
        frames / jnp.sqrt(jnp.sum(frames * frames, axis=-1, keepdims=True) + 1e-06)
    ).astype(jnp.bfloat16)
    scale_value = logit_scale[0]
    own_pair = scale_value * jnp.sum(
        embed_unit.astype(jnp.float32) * frame_unit.astype(jnp.float32), axis=-1
    )
    smallest_value = jnp.full((clips_here,), -jnp.inf, jnp.float32)
    nothing = jnp.zeros((clips_here,), jnp.float32)
    row_top = smallest_value
    row_sum = nothing
    col_top = smallest_value
    col_sum = nothing
    other_embed = lax.all_gather(embed_unit, ("sess", "dp", "fsdp"), axis=0, tiled=True)
    other_frame = lax.all_gather(frame_unit, ("sess", "dp", "fsdp"), axis=0, tiled=True)
    row_logit = scale_value * jnp.dot(embed_unit, other_frame.T, preferred_element_type=jnp.float32)
    col_logit = scale_value * jnp.dot(frame_unit, other_embed.T, preferred_element_type=jnp.float32)
    row_next = jnp.max(row_logit, axis=1)
    col_next = jnp.max(col_logit, axis=1)
    row_sum = row_sum * jnp.exp(row_top - row_next) + jnp.sum(
        jnp.exp(row_logit - row_next[:, None]), axis=1
    )
    col_sum = col_sum * jnp.exp(col_top - col_next) + jnp.sum(
        jnp.exp(col_logit - col_next[:, None]), axis=1
    )
    row_top, row_sum, col_top, col_sum = (row_next, row_sum, col_next, col_sum)
    clip_loss = 0.5 * (row_top + jnp.log(row_sum) + col_top + jnp.log(col_sum)) - own_pair
    return (latent_state, clip_loss)


def solution(mesh):
    return jax.shard_map(
        per_device,
        mesh=mesh,
        in_specs=(
            P(("sess", "dp", "fsdp"), None, None),
            P(("sess", "dp", "fsdp"), None),
            P(("sess", "dp", "fsdp")),
            P(("sess", "dp", "fsdp")),
            P(),
            P(),
            P("fsdp", None),
            P("fsdp", None),
            P("fsdp", None),
            P(),
            P(("sess", "dp", "fsdp")),
            P(),
        ),
        out_specs=(P(("sess", "dp", "fsdp"), None, None), P(("sess", "dp", "fsdp"))),
        check_vma=False,
    )
```

profile of v0, /device:TPU:1, one launch (start us, length us, event | category | flops | bytes accessed | tf_op | source)
XLA Modules:
  0.0 1874.7 jit_solution(8112834568392189841)
XLA Ops:
  11.1 12.7 all-to-all-start
  23.9 4.8 reshape.604
  28.7 7.1 fusion.134
  35.8 31.8 %copy.220 = bf16[32,2,131072]{2,1,0:T(2,128)(2,1)} copy(bf16[32,2,131072]{2,0,1:T(8,128)(2,1)S(1)} %fusion.134) | data formatting | bytes 33554432 | tf_op jit(solution)/shard_map/bs,bx->sx/dot_general | solution.py:63
  67.6 10.0 all-to-all-start.1
  82.2 358.1 %all-to-all-done.1 = bf16[32,2,131072]{2,1,0:T(2,128)(2,1)} async-done(((bf16[32,2,131072]{2,1,0:T(2,128)(2,1)}), bf16[32,2,131072]{2,1,0:T(2,128)(2,1)}, u32[]{:S(2)}, u32[]{:S(2)}) %all-to-all-start.1) | async-done | bytes 16777248 | tf_op jit(solution)/shard_map/all_to_all | solution.py:71
  440.3 29.1 %reshape.408 = bf16[8192,1024]{1,0:T(8,128)(2,1)} reshape(bf16[32,2,131072]{2,1,0:T(2,128)(2,1)} %all-to-all-done.1) | data formatting | bytes 33554432 | tf_op jit(solution)/shard_map/reshape | solution.py:74
  469.4 12.7 convolution_convert_fusion
  482.1 3.6 fusion.167
  485.8 6.6 copy.310
  492.4 1.7 fusion.185
  494.2 1.7 fusion.171
  496.0 2.7 fusion.172
  498.7 2.6 fusion.173
  501.3 2.6 fusion.174
  504.0 2.6 fusion.175
  506.6 2.6 fusion.176
  509.3 2.6 fusion.177
  511.9 2.6 fusion.178
  514.6 2.6 fusion.179
  517.3 2.6 fusion.180
  519.9 2.6 fusion.181
  522.6 2.6 fusion.182
  525.2 2.6 fusion.183
  527.9 2.6 fusion.184
  530.5 2.6 fusion.170
  543.1 6.8 copy.308
  550.1 2.0 fusion.99
  552.1 3.3 convolution_bitcast_fusion
  556.0 1.7 convolution_bitcast_fusion.1
  558.4 1.7 convolution_bitcast_fusion.2
  560.8 1.7 convolution_bitcast_fusion.3
  563.1 1.7 convolution_bitcast_fusion.4
  565.5 1.7 convolution_bitcast_fusion.5
  567.9 1.8 convolution_bitcast_fusion.6
  570.3 1.7 convolution_bitcast_fusion.7
  572.7 1.7 convolution_bitcast_fusion.8
  575.0 1.9 convolution_bitcast_fusion.9
  577.6 1.7 convolution_bitcast_fusion.10
  580.0 1.7 convolution_bitcast_fusion.11
  582.3 1.7 convolution_bitcast_fusion.12
  584.7 1.7 convolution_bitcast_fusion.13
  587.0 1.8 convolution_bitcast_fusion.14
  592.6 2.3 fusion.52
  594.9 2.3 fusion.51
  597.2 1.0 fusion.50
  598.3 2.3 fusion.49
  600.6 2.5 fusion.48
  603.1 2.3 fusion.47
  605.4 2.3 fusion.46
  607.7 2.2 fusion.45
  609.9 1.0 fusion.44
  611.0 1.0 fusion.43
  612.1 1.0 fusion.42
  613.1 1.0 fusion.41
  614.2 1.0 fusion.40
  615.2 1.0 fusion.39
  616.3 1.0 fusion.38
  617.3 2.0 convolution_bitcast_fusion.15
  619.3 1.3 fusion.37
  621.4 2.7 fusion.168
  624.1 1.6 multiply_reduce_fusion.17
  625.9 618.2 %all-gather = bf16[256,2,512]{2,1,0:T(2,128)(2,1)S(1)} all-gather(bf16[1,2,512]{2,1,0:T(2,128)(2,1)S(1)} %bitcast.394), channel_id=1, replica_groups=mesh['sess'=32,'dp'=4,'fsdp'=2] {'sess','dp','fsdp'}, dimensions={0}, use_global_device_ids=true | all-gather | bytes 526336 | tf_op jit(solution)/shard_map/all_gather | solution.py:146
  1244.3 621.6 %all-gather.1 = bf16[256,2,512]{2,1,0:T(2,128)(2,1)S(1)} all-gather(bf16[1,2,512]{2,1,0:T(2,128)(2,1)S(1)} %bitcast.395), channel_id=1, replica_groups=mesh['sess'=32,'dp'=4,'fsdp'=2] {'sess','dp','fsdp'}, dimensions={0}, use_global_device_ids=true | all-gather | bytes 526336 | tf_op jit(solution)/shard_map/all_gather | solution.py:145
  (215 shorter events, 34.5 us)
Async XLA Ops:
  7.2 73.5 %copy-start = (bf16[512,512]{1,0:T(8,128)(2,1)S(1)}, bf16[512,512]{1,0:T(8,128)(2,1)}, u32[]{:S(2)}) copy-start(bf16[512,512]{1,0:T(8,128)(2,1)} %param.23) | copy-start | bytes 1572868
  11.1 56.5 %all-to-all-start = ((bf16[32,2,2]{1,2,0:T(2,128)(2,1)}), bf16[32,2,2]{1,2,0:T(2,128)(2,1)S(1)}, u32[]{:S(2)}, u32[]{:S(2)}) async-start(bf16[32,2,2]{1,2,0:T(2,128)(2,1)} %copy.217), calls=%async_computation | async-start | bytes 32768 | tf_op jit(solution)/shard_map/all_to_all | solution.py:72
  67.6 12.3 copy-start.24
  67.6 12.4 copy-start.25
  67.6 13.1 copy-start.26
  67.6 372.8 %all-to-all-start.1 = ((bf16[32,2,131072]{2,1,0:T(2,128)(2,1)}), bf16[32,2,131072]{2,1,0:T(2,128)(2,1)}, u32[]{:S(2)}, u32[]{:S(2)}) async-start(bf16[32,2,131072]{2,1,0:T(2,128)(2,1)} %copy.220), calls=%async_computation.1 | async-start | bytes 33554432 | tf_op jit(solution)/shard_map/all_to_all | solution.py:71
  77.6 391.8 %all-gather.6.cloned.1.call-start = ((), (), s32[]{:S(2)}) async-start(), calls=%async_computation.2 | async-start | bytes 1572864 | tf_op jit(solution)/shard_map/all_gather | solution.py:18
  78.3 543.0 %all-gather.8.cloned.1.call-start = ((), (), s32[]{:S(2)}) async-start(), calls=%async_computation.3 | async-start | bytes 3145728 | tf_op jit(solution)/shard_map/all_gather | solution.py:22
  79.1 545.0 %all-gather.10.cloned.1.call-start = ((), (), s32[]{:S(2)}) async-start(), calls=%async_computation.4 | async-start | bytes 1572864 | tf_op jit(solution)/shard_map/all_gather | solution.py:26
  549.9 5.4 copy-start.15
  549.9 6.1 copy-start.2
  550.0 7.7 copy-start.14
  555.3 4.8 copy-start.13
  557.7 4.7 copy-start.12
  560.1 4.7 copy-start.11
  562.5 4.8 copy-start.10
  564.9 4.8 copy-start.9
  567.2 4.8 copy-start.8
  569.7 4.7 copy-start.7
  572.0 5.0 copy-start.6
  574.4 5.0 copy-start.5
  577.0 4.7 copy-start.4
  579.3 4.7 copy-start.3
  588.8 8.4 copy-start.16
  592.6 17.4 copy-start.17
  594.9 16.1 copy-start.18
  597.2 14.8 copy-start.19
  598.3 14.8 copy-start.20
  600.6 13.6 copy-start.21
  603.1 12.1 copy-start.22
  605.4 10.9 copy-start.23
  619.3 1248.5 %copy-start.1 = (bf16[512,512]{1,0:T(8,128)(2,1)S(1)}, bf16[512,512]{1,0:T(8,128)(2,1)}, u32[]{:S(2)}) copy-start(bf16[512,512]{1,0:T(8,128)(2,1)} %param.23) | copy-start | bytes 1572868
Sparse Core Ops, SparseCore 0:
  80.2 53.6 all-gather.5
  135.7 57.1 all-gather.7
  194.7 53.7 all-gather.9
where the time goes:
time: 1900 us; the launch traced here: 1870 us
  blocking collectives  1240 us (65%)
  waiting for transfers between devices  360 us (19%)
  matrix products  120 us (6%)
  local copies, waits for them, and re-layouts  99.2 us (5%)
  starting transfers between devices  22.9 us (1%)
    all_gather x1, blocking collectives, per_device(): lax.all_gather(embed_unit, ('sess', 'dp', 'fsdp'), axis=0, tiled=True)  622 us
    all_gather x1, blocking collectives, per_device(): lax.all_gather(frame_unit, ('sess', 'dp', 'fsdp'), axis=0, tiled=True)  618 us
    all_to_all x1, waiting for transfers between devices, per_device(): lax.all_to_all(packed, 'sess', split_axis=0, concat_axis=0, tiled=True)  358 us
    dot_general x16, matrix products, per_device(): jnp.einsum('wa,pha->wph', query[:, head_position], keys[:, :, key_value_h...  39.7 us
  transfers between devices with their start and end apart: 5, of which 1 were waited for; matrix products, arithmetic and copies ran while one was open for 12% of the time, Pallas kernels for 0%

commit v1 on v0

v1 whole, which is shorter than its diff:
```python
import jax
import jax.numpy as jnp
from jax import lax
from jax.experimental import pallas as pl
from jax.experimental.pallas import tpu as pltpu
from jax.sharding import PartitionSpec as P

HEADS = 16
HEAD_DIM = 64
KV_HEADS = 4
GROUP = HEADS // KV_HEADS
NZ = 8
NY = 2
NC = 2
PEERS = NY * NZ * NC
F32 = jnp.float32
BF16 = jnp.bfloat16
MESH = pl.DeviceIdType.MESH
VMEM_SPEC = pl.BlockSpec(memory_space=pltpu.VMEM)
SMEM_SPEC = pl.BlockSpec(memory_space=pltpu.SMEM)


def place():
    sess = lax.axis_index("sess")
    y_hi = sess // (NZ * NC)
    z = (sess // NC) % NZ
    core = sess % NC
    return sess, y_hi, z, core


def sess_of(y_hi, z, core):
    return (y_hi * NZ + z) * NC + core


def remote(src, dst, send_sem, recv_sem, where):
    return pltpu.make_async_remote_copy(
        src_ref=src, dst_ref=dst, send_sem=send_sem, recv_sem=recv_sem, device_id=where, device_id_type=MESH
    )


def weight_peers():
    sess, y_hi, z, core = place()
    half = lax.axis_index("fsdp")
    near = {"sess": sess, "fsdp": 1 - half}
    far = {"sess": sess_of(1 - y_hi, z, core), "fsdp": 1 - half}
    twin = {"sess": sess_of(y_hi, z, 1 - core)}
    return half, core, near, far, twin


def weight_copies(src, out, send, recv):
    half, core, near, far, twin = weight_peers()
    first = [
        remote(src.at[2 * core + i], out.at[half, 2 * core + i], send.at[i], recv.at[i], to)
        for i, to in enumerate((near, far))
    ]
    relay = [
        remote(
            out.at[1 - half, 2 * core + i], out.at[1 - half, 2 * core + i], send.at[2 + i], recv.at[2 + i], twin
        )
        for i in range(2)
    ]
    return first, relay


def kv_weight_kernel(w_ref, out_ref, send, recv, local):
    half, core, near, far, twin = weight_peers()
    barrier = pltpu.get_barrier_semaphore()
    for to in (near, far, twin):
        pl.semaphore_signal(barrier, inc=1, device_id=to, device_id_type=MESH)
    own = pltpu.make_async_copy(w_ref, out_ref.at[half], local)
    own.start()
    pl.semaphore_wait(barrier, 3)
    first, relay = weight_copies(w_ref, out_ref, send, recv)
    for c in first:
        c.start()
    for c, r in zip(first, relay):
        c.wait_recv()
        r.start()
    for r in relay:
        r.wait_recv()
    for c in first + relay:
        c.wait_send()
    own.wait()


def gather_kv_weight(w):
    rows, cols = w.shape
    quarter = rows // 4
    out = pl.pallas_call(
        kv_weight_kernel,
        name="kv_weight",
        out_shape=jax.ShapeDtypeStruct((2, 4, quarter, cols), w.dtype),
        in_specs=[VMEM_SPEC],
        out_specs=VMEM_SPEC,
        scratch_shapes=[
            pltpu.SemaphoreType.DMA((4,)),
            pltpu.SemaphoreType.DMA((4,)),
            pltpu.SemaphoreType.DMA,
        ],
        compiler_params=pltpu.CompilerParams(collective_id=0, has_side_effects=True),
    )(w.reshape(4, quarter, cols))
    return out.reshape(2 * rows, cols)


def project_kernel(per, owner, clip, valid, x_ref, w_ref, q_ref, kv_ref, tops_ref, qt_ref):
    step = pl.program_id(0)
    rows = x_ref.shape[1]
    lat = q_ref.shape[0]

    @pl.when(step == 0)
    def _():
        tops_ref[...] = jnp.zeros_like(tops_ref)
        qt_ref[...] = jnp.zeros_like(qt_ref)
        qt = (q_ref[...].astype(F32) * (HEAD_DIM**-0.5)).T.astype(BF16)
        for head in range(HEADS):
            kh, j = head // GROUP, head % GROUP
            pair, inner = kh // 2, kh % 2
            qt_ref[
                pair,
                inner * HEAD_DIM : (inner + 1) * HEAD_DIM,
                inner * GROUP * lat + j * lat : inner * GROUP * lat + (j + 1) * lat,
            ] = qt[head * HEAD_DIM : (head + 1) * HEAD_DIM, :]

    kv = jnp.dot(x_ref[...].reshape(per * rows, x_ref.shape[2]), w_ref[...], preferred_element_type=F32)
    kv = kv.astype(BF16)
    kv_ref[...] = kv.reshape(per, rows, kv.shape[1])
    row = lax.broadcasted_iota(jnp.int32, (rows, 1), 0)
    for pair in range(2):
        scores = jnp.dot(kv[:, pair * 128 : (pair + 1) * 128], qt_ref[pair], preferred_element_type=F32)
        for i in range(per):
            block = step * per + i
            slot = owner[block] * 2 + clip[block]
            part = scores[i * rows : (i + 1) * rows, :]
            top = jnp.max(jnp.where(row < valid[block], part, 0.0), axis=0, keepdims=True)
            for inner in range(2):
                kh = pair * 2 + inner
                now = tops_ref[slot, kh : kh + 1, :]
                tops_ref[slot, kh : kh + 1, :] = jnp.maximum(now, top[:, inner * 128 : (inner + 1) * 128])


def project(owner, clip, valid, x, w, q):
    blocks, rows, width = x.shape
    cols = w.shape[1]
    per = 2
    return pl.pallas_call(
        lambda *refs: project_kernel(per, *refs),
        name="project",
        grid_spec=pltpu.PrefetchScalarGridSpec(
            num_scalar_prefetch=3,
            grid=(blocks // per,),
            in_specs=[
                pl.BlockSpec((per, rows, width), lambda i, *_: (i, 0, 0)),
                pl.BlockSpec((width, cols), lambda i, *_: (0, 0)),
                pl.BlockSpec(q.shape, lambda i, *_: (0, 0)),
            ],
            out_specs=[
                pl.BlockSpec((per, rows, cols), lambda i, *_: (i, 0, 0)),
                pl.BlockSpec((PEERS * 2, 4, 128), lambda i, *_: (0, 0, 0)),
                pl.BlockSpec((2, 128, 256), lambda i, *_: (0, 0, 0)),
            ],
        ),
        out_shape=[
            jax.ShapeDtypeStruct((blocks, rows, cols), BF16),
            jax.ShapeDtypeStruct((PEERS * 2, 4, 128), F32),
            jax.ShapeDtypeStruct((2, 128, 256), BF16),
        ],
    )(owner, clip, valid, x, w, q)


def tops_kernel(mine_ref, all_ref, own_ref, inbox, send, recv, send2, recv2):
    sess, *_ = place()
    barrier = pltpu.get_barrier_semaphore()

    def signal(k, _):
        pl.semaphore_signal(
            barrier, inc=1, device_id={"sess": lax.rem(sess + k, PEERS)}, device_id_type=MESH
        )
        return _

    lax.fori_loop(1, PEERS, signal, 0)
    pl.semaphore_wait(barrier, PEERS - 1)

    def copy_in(k):
        to = lax.rem(sess + k, PEERS)
        return remote(mine_ref.at[to], inbox.at[k], send.at[k], recv.at[k], {"sess": to})

    def copy_out(k):
        to = lax.rem(sess + k, PEERS)
        return remote(own_ref, all_ref.at[sess], send2.at[k], recv2.at[k], {"sess": to})

    def arrival(k):
        source = lax.rem(sess + PEERS - k, PEERS)
        return remote(own_ref, all_ref.at[source], send2.at[k], recv2.at[k], {"sess": source})

    def start(k, _):
        copy_in(k).start()
        return _

    lax.fori_loop(1, PEERS, start, 0)

    def gather(k, top):
        copy_in(k).wait_recv()
        return jnp.maximum(top, inbox[k])

    top = lax.fori_loop(1, PEERS, gather, mine_ref[sess])
    own_ref[...] = top

    def start2(k, _):
        copy_out(k).start()
        return _

    lax.fori_loop(1, PEERS, start2, 0)
    all_ref[sess] = top

    def finish(k, _):
        copy_in(k).wait_send()
        copy_out(k).wait_send()
        arrival(k).wait_recv()
        return _

    lax.fori_loop(1, PEERS, finish, 0)


def exchange_tops(tops):
    return pl.pallas_call(
        tops_kernel,
        name="tops",
        out_shape=[
            jax.ShapeDtypeStruct((PEERS, 2, 4, 128), F32),
            jax.ShapeDtypeStruct((2, 4, 128), F32),
        ],
        in_specs=[VMEM_SPEC],
        out_specs=[VMEM_SPEC, VMEM_SPEC],
        scratch_shapes=[pltpu.VMEM((PEERS, 2, 4, 128), F32)] + [pltpu.SemaphoreType.DMA((PEERS,))] * 4,
        compiler_params=pltpu.CompilerParams(collective_id=1, has_side_effects=True),
    )(tops.reshape(PEERS, 2, 4, 128))


SUB = 264


def weigh_kernel(per, owner, clip, valid, kv_ref, tops_ref, qt_ref, out_ref):
    step = pl.program_id(0)
    rows = kv_ref.shape[1]

    @pl.when(step == 0)
    def _():
        out_ref[...] = jnp.zeros_like(out_ref)

    row = lax.broadcasted_iota(jnp.int32, (rows, 1), 0)
    for i in range(per):
        block = step * per + i
        who = owner[block]
        y_hi, z, core = who // (NZ * NC), (who // NC) % NZ, who % NC
        slot = ((core * NZ + z) * NY + y_hi) * 2 + clip[block]
        live = row < valid[block]
        for pair in range(2):
            scores = jnp.dot(
                kv_ref[i, :, pair * 128 : (pair + 1) * 128], qt_ref[pair], preferred_element_type=F32
            )
            values = kv_ref[i, :, 256 + pair * 128 : 256 + (pair + 1) * 128].astype(F32).T.astype(BF16)
            for inner in range(2):
                kh = pair * 2 + inner
                top = tops_ref[who * 2 + clip[block], kh : kh + 1, :]
                prob = jnp.where(live, jnp.exp(scores[:, inner * 128 : (inner + 1) * 128] - top), 0.0)
                total = jnp.sum(prob, axis=0, keepdims=True)
                part = jnp.dot(
                    values[inner * HEAD_DIM : (inner + 1) * HEAD_DIM, :],
                    prob.astype(BF16),
                    preferred_element_type=F32,
                )
                out_ref[slot, kh * HEAD_DIM : (kh + 1) * HEAD_DIM, :] += part
                out_ref[slot, 256 + kh : 257 + kh, :] += total


def weigh(owner, clip, valid, kv, tops, qt):
    blocks, rows, cols = kv.shape
    per = 2
    return pl.pallas_call(
        lambda *refs: weigh_kernel(per, *refs),
        name="weigh",
        grid_spec=pltpu.PrefetchScalarGridSpec(
            num_scalar_prefetch=3,
            grid=(blocks // per,),
            in_specs=[
                pl.BlockSpec((per, rows, cols), lambda i, *_: (i, 0, 0)),
                pl.BlockSpec((PEERS * 2, 4, 128), lambda i, *_: (0, 0, 0)),
                pl.BlockSpec((2, 128, 256), lambda i, *_: (0, 0, 0)),
            ],
            out_specs=pl.BlockSpec((PEERS * 2, SUB, 128), lambda i, *_: (0, 0, 0)),
        ),
        out_shape=jax.ShapeDtypeStruct((PEERS * 2, SUB, 128), F32),
    )(owner, clip, valid, kv, tops, qt)


ORDER = (4, 3, 5, 2, 6, 1, 7, 0)


def reduce_kernel(
    part_ref, wo_ref, wp_ref, out_ref, wo_out, wp_out,
    twin_in, run, chain_in, y_in, final,
    csend, crecv, zsend, zrecv, ysend, yrecv, wsend, wrecv, local,
):
    sess, y_hi, z, core = place()
    half, _, near, far, twin = weight_peers()
    up = {"sess": sess_of(y_hi, lax.rem(z + 1, NZ), core)}
    down = {"sess": sess_of(y_hi, lax.rem(z + NZ - 1, NZ), core)}
    across = {"sess": sess_of(1 - y_hi, z, core)}
    barrier = pltpu.get_barrier_semaphore()
    for to in (near, far, twin, up, down, across):
        pl.semaphore_signal(barrier, inc=1, device_id=to, device_id_type=MESH)
    owns = [
        pltpu.make_async_copy(wo_ref, wo_out.at[half], local.at[0]),
        pltpu.make_async_copy(wp_ref, wp_out.at[half], local.at[1]),
    ]
    for c in owns:
        c.start()
    pl.semaphore_wait(barrier, 6)

    to_twin = {}
    for k in ORDER:
        dest = lax.rem(z + k, NZ)
        to_twin[k] = remote(part_ref.at[1 - core, dest], twin_in.at[k], csend.at[k], crecv.at[k], twin)
        to_twin[k].start()
    weights = []
    for i, (src, out) in enumerate(((wo_ref, wo_out), (wp_ref, wp_out))):
        weights.append(weight_copies(src, out, wsend.at[i], wrecv.at[i]))
        for c in weights[i][0]:
            c.start()

    sent = {}
    ways = (up, down)

    def own_sum(k, sub):
        return part_ref[core, lax.rem(z + k, NZ), sub] + twin_in[k, sub]

    def pass_on(way, hop, sub, value):
        run[way, hop, sub] = value
        c = remote(
            run.at[way, hop, sub],
            chain_in.at[way, hop, sub],
            zsend.at[way, hop, sub],
            zrecv.at[way, hop, sub],
            ways[way],
        )
        c.start()
        sent[way, hop, sub] = c

    to_twin[4].wait_recv()
    for sub in range(2):
        pass_on(0, 0, sub, own_sum(4, sub))
        pass_on(1, 0, 2 + sub, own_sum(4, 2 + sub))
    for hop in range(1, 4):
        ks = (4 - hop, NZ - (4 - hop))
        for k in ks:
            to_twin[k].wait_recv()
        for turn in range(4):
            for way in range(2):
                sub = (turn + 2) % 4 if way == 0 else turn
                value = own_sum(ks[way], sub)
                if (way, hop - 1, sub) in sent:
                    sent[way, hop - 1, sub].wait_recv()
                    value = value + chain_in[way, hop - 1, sub]
                pass_on(way, hop, sub, value)
        if hop == 1:
            for first, relay in weights:
                for c, r in zip(first, relay):
                    c.wait_recv()
                    r.start()

    to_twin[0].wait_recv()
    for sub in range(4):
        value = own_sum(0, sub)
        for way in range(2):
            sent[way, 3, sub].wait_recv()
            value = value + chain_in[way, 3, sub]
        final[sub] = value
    over = []
    for i in range(2):
        c = remote(final.at[(1 - y_hi) * 2 + i], y_in.at[i], ysend.at[i], yrecv.at[i], across)
        c.start()
        over.append(c)
    for i in range(2):
        over[i].wait_recv()
        out_ref[i] = final[y_hi * 2 + i] + y_in[i]

    for c in over:
        c.wait_send()
    for c in sent.values():
        c.wait_send()
    for c in to_twin.values():
        c.wait_send()
    for first, relay in weights:
        for r in relay:
            r.wait_recv()
        for c in first + relay:
            c.wait_send()
    for c in owns:
        c.wait()


def reduce_to_owner(parts, w_out, w_proj):
    wo = w_out.reshape(4, w_out.shape[0] // 4, w_out.shape[1])
    wp = w_proj.reshape(4, w_proj.shape[0] // 4, w_proj.shape[1])
    dma = pltpu.SemaphoreType.DMA
    sums, wo_all, wp_all = pl.pallas_call(
        reduce_kernel,
        name="reduce",
        out_shape=[
            jax.ShapeDtypeStruct((2, SUB, 128), F32),
            jax.ShapeDtypeStruct((2,) + wo.shape, wo.dtype),
            jax.ShapeDtypeStruct((2,) + wp.shape, wp.dtype),
        ],
        in_specs=[VMEM_SPEC] * 3,
        out_specs=[VMEM_SPEC] * 3,
        scratch_shapes=[
            pltpu.VMEM((NZ, 4, SUB, 128), F32),
            pltpu.VMEM((2, 4, 4, SUB, 128), F32),
            pltpu.VMEM((2, 4, 4, SUB, 128), F32),
            pltpu.VMEM((2, SUB, 128), F32),
            pltpu.VMEM((4, SUB, 128), F32),
            dma((NZ,)),
            dma((NZ,)),
            dma((2, 4, 4)),
            dma((2, 4, 4)),
            dma((2,)),
            dma((2,)),
            dma((2, 4)),
            dma((2, 4)),
            dma((2,)),
        ],
        compiler_params=pltpu.CompilerParams(collective_id=2, has_side_effects=True),
    )(parts.reshape(NC, NZ, NY * 2, SUB, 128), wo, wp)
    return sums, wo_all.reshape(-1, w_out.shape[1]), wp_all.reshape(-1, w_proj.shape[1])


def embed_kernel(
    frame, scale, sums_ref, top_ref, lat_ref, wo_ref, wp_ref, movie_ref, state_ref, msg_ref, logit_ref, pick_ref, attn
):
    lat = lat_ref.shape[0]
    for c in range(2):
        columns = []
        for kh in range(KV_HEADS):
            total = sums_ref[c, 256 + kh : 257 + kh, :] + jnp.exp(-top_ref[c, kh : kh + 1, :])
            columns.append(sums_ref[c, kh * HEAD_DIM : (kh + 1) * HEAD_DIM, :] / total)
        turned = jnp.concatenate(columns, axis=0).T.astype(BF16)
        for head in range(HEADS):
            kh, j = head // GROUP, head % GROUP
            attn[c * lat : (c + 1) * lat, head * HEAD_DIM : (head + 1) * HEAD_DIM] = turned[
                j * lat : (j + 1) * lat, kh * HEAD_DIM : (kh + 1) * HEAD_DIM
            ]
    mixed = jnp.dot(attn[...], wo_ref[...], preferred_element_type=F32)
    row = lax.broadcasted_iota(jnp.int32, (16, 1), 0)
    pooled = jnp.zeros((16, mixed.shape[1]), F32)
    for c in range(2):
        state = lat_ref[...].astype(F32) + mixed[c * lat : (c + 1) * lat]
        state_ref[c] = state.astype(BF16)
        pooled = jnp.where(row == c, jnp.mean(state, axis=0, keepdims=True), pooled)
    z = jnp.dot(pooled.astype(BF16), wp_ref[...], preferred_element_type=F32)
    zn = (z / jnp.sqrt(jnp.sum(z * z, axis=-1, keepdims=True) + 1e-06)).astype(BF16)
    movie = movie_ref[...].astype(F32)
    tn = (movie / jnp.sqrt(jnp.sum(movie * movie, axis=-1, keepdims=True) + 1e-06)).astype(BF16)
    logits = lax.dot_general(zn, tn, (((1,), (1,)), ((), ())), preferred_element_type=F32) * scale[0]
    lane = lax.broadcasted_iota(jnp.int32, (1, 128), 1)
    for r in range(4):
        piece = logits[:, r * 128 : (r + 1) * 128]
        msg_ref[r : r + 1, :] = jnp.exp(piece[0:1]) + jnp.exp(piece[1:2])
        picks = []
        for c in range(2):
            picks.append((lane + r * 128 == frame[c]).astype(F32))
            logit_ref[c * 4 + r : c * 4 + r + 1, :] = piece[c : c + 1]
            pick_ref[c * 4 + r : c * 4 + r + 1, :] = picks[c]
        msg_ref[4 + r : 5 + r, :] = picks[0] + picks[1]


def embed(frame, scale, sums, top, latents, w_out, w_proj, movie):
    lat, width = latents.shape
    small = jax.ShapeDtypeStruct((8, 128), F32)
    return pl.pallas_call(
        embed_kernel,
        name="embed",
        out_shape=[jax.ShapeDtypeStruct((2, lat, width), BF16), small, small, small],
        in_specs=[SMEM_SPEC, SMEM_SPEC] + [VMEM_SPEC] * 6,
        out_specs=[VMEM_SPEC] * 4,
        scratch_shapes=[pltpu.VMEM((2 * lat, width), BF16)],
    )(frame, scale, sums, top, latents, w_out, w_proj, movie)


def loss_kernel(msg_ref, logit_ref, pick_ref, out_ref, inbox, inbox2, column, send, recv, send2, recv2):
    sess, y_hi, z, core = place()
    x, half = lax.axis_index("dp"), lax.axis_index("fsdp")
    spots = NY * NC * 4 * 2
    here = ((y_hi * NC + core) * 4 + x) * 2 + half

    def along(k):
        return {"sess": sess_of(y_hi, lax.rem(z + k, NZ), core)}

    def plane(k):
        at = lax.rem(here + k, spots)
        return {
            "sess": sess_of(at // (NC * 8), z, (at // 8) % NC),
            "dp": (at // 2) % 4,
            "fsdp": at % 2,
        }

    barrier = pltpu.get_barrier_semaphore()

    def signal_z(k, _):
        pl.semaphore_signal(barrier, inc=1, device_id=along(k), device_id_type=MESH)
        return _

    def signal_p(k, _):
        pl.semaphore_signal(barrier, inc=1, device_id=plane(k), device_id_type=MESH)
        return _

    lax.fori_loop(1, NZ, signal_z, 0)
    lax.fori_loop(1, spots, signal_p, 0)
    pl.semaphore_wait(barrier, NZ - 1 + spots - 1)

    def copy_z(k):
        return remote(msg_ref, inbox.at[k], send.at[k], recv.at[k], along(k))

    def copy_p(k):
        return remote(column, inbox2.at[k], send2.at[k], recv2.at[k], plane(k))

    def start_z(k, _):
        copy_z(k).start()
        return _

    def add_z(k, total):
        copy_z(k).wait_recv()
        return total + inbox[k]

    def start_p(k, _):
        copy_p(k).start()
        return _

    def add_p(k, total):
        copy_p(k).wait_recv()
        return total + inbox2[k]

    lax.fori_loop(1, NZ, start_z, 0)
    total = lax.fori_loop(1, NZ, add_z, msg_ref[...])
    column[...] = total
    lax.fori_loop(1, spots, start_p, 0)
    total = lax.fori_loop(1, spots, add_p, total)

    def whole(v):
        return jnp.sum(jnp.sum(v, axis=1, keepdims=True), axis=0, keepdims=True)

    for c in range(2):
        logit, pick = logit_ref[c * 4 : c * 4 + 4, :], pick_ref[c * 4 : c * 4 + 4, :]
        row_sum = whole(total[4:8] * jnp.exp(logit))
        col_sum = whole(total[0:4] * pick)
        loss = 0.5 * (jnp.log(row_sum) + jnp.log(col_sum)) - whole(logit * pick)
        out_ref[c : c + 1, :] = jnp.broadcast_to(loss, (1, 128))

    def end_z(k, _):
        copy_z(k).wait_send()
        return _

    def end_p(k, _):
        copy_p(k).wait_send()
        return _

    lax.fori_loop(1, NZ, end_z, 0)
    lax.fori_loop(1, spots, end_p, 0)


def clip_losses(msg, logits, picks):
    dma = pltpu.SemaphoreType.DMA
    spots = NY * NC * 8
    return pl.pallas_call(
        loss_kernel,
        name="loss",
        out_shape=jax.ShapeDtypeStruct((2, 128), F32),
        in_specs=[VMEM_SPEC] * 3,
        out_specs=VMEM_SPEC,
        scratch_shapes=[
            pltpu.VMEM((NZ, 8, 128), F32),
            pltpu.VMEM((spots, 8, 128), F32),
            pltpu.VMEM((8, 128), F32),
            dma((NZ,)),
            dma((NZ,)),
            dma((spots,)),
            dma((spots,)),
        ],
        compiler_params=pltpu.CompilerParams(collective_id=3, has_side_effects=True),
    )(msg, logits, picks)


def per_device(
    unit_tokens,
    block_owner,
    block_clip,
    block_valid,
    latent_query_rows,
    latents,
    w_kv,
    w_out,
    w_proj,
    movie_frame_embeddings,
    clip_frame,
    logit_scale,
):
    owner = block_owner.reshape(-1)
    weight = gather_kv_weight(w_kv)
    kv, tops, qt = project(owner, block_clip, block_valid, unit_tokens, weight, latent_query_rows)
    all_tops, own_top = exchange_tops(tops)
    parts = weigh(owner, block_clip, block_valid, kv, all_tops.reshape(PEERS * 2, 4, 128), qt)
    sums, wo, wp = reduce_to_owner(parts, w_out, w_proj)
    state, msg, logits, picks = embed(
        clip_frame, logit_scale, sums, own_top, latents, wo, wp, movie_frame_embeddings
    )
    loss = clip_losses(msg, logits, picks)
    return state, loss[:, 0]


def solution(mesh):
    return jax.shard_map(
        per_device,
        mesh=mesh,
        in_specs=(
            P(("sess", "dp", "fsdp"), None, None),
            P(("sess", "dp", "fsdp"), None),
            P(("sess", "dp", "fsdp")),
            P(("sess", "dp", "fsdp")),
            P(),
            P(),
            P("fsdp", None),
            P("fsdp", None),
            P("fsdp", None),
            P(),
            P(("sess", "dp", "fsdp")),
            P(),
        ),
        out_specs=(P(("sess", "dp", "fsdp"), None, None), P(("sess", "dp", "fsdp"))),
        check_vma=False,
    )
```

time: 1900 us -> 143 us (0.08); the launches traced: 1870 us -> 142 us
  blocking collectives: 1240 us -> 0 us
  waiting for transfers between devices: 360 us -> 0 us
  Pallas kernels: 0 us -> 140 us
  matrix products: 120 us -> 0 us
  local copies, waits for them, and re-layouts: 99.2 us -> 1.26 us
  starting transfers between devices: 22.9 us -> 0 us
    all_gather x2 -> x0, blocking collectives: 1240 us -> none  [the longest x1 622 us: per_device(): lax.all_gather(embed_unit, ('sess', 'dp', 'fsdp'), axis=0, tiled=True)]
    all_to_all x2 -> x0, waiting for transfers between devices: 358 us -> none  [the longest x1 358 us: per_device(): lax.all_to_all(packed, 'sess', split_axis=0, concat_axis=0, tiled=True)]
    pallas_call x0 -> x7, Pallas kernels: none -> 140 us  [the longest x1 61.4 us: reduce_to_owner(): pl.pallas_call(reduce_kernel, name='reduce', out_shape=[jax.ShapeDtypeStr...]
    dot_general x55 -> x0, matrix products: 120 us -> none  [the longest x16 39.7 us: per_device(): jnp.einsum('wa,pha->wph', query[:, head_position], keys[:, :, key_value_h...]
    reshape x7 -> x0, local copies, waits for them, and re-layouts: 35 us -> none  [the longest x1 29.1 us: per_device(): arrived.reshape(slots_all * block_rows, width)]
    dot_general x1 -> x0, local copies, waits for them, and re-layouts: 31.8 us -> none  [per_device(): jnp.einsum('bs,bx->sx', placing, unit_tokens.reshape(blocks_here, block_r...]
    all_to_all x2 -> x0, starting transfers between devices: 22.8 us -> none  [the longest x1 12.7 us: per_device(): lax.all_to_all(slot_meta, 'sess', split_axis=0, concat_axis=0, tiled=True)]
  transfers between devices with their start and end apart: 5 -> 0, of which waited for: 1 -> 0; matrix products, arithmetic and copies ran while one was open for 12% -> 0% of each run, Pallas kernels for 0% -> 0%
where the time goes in v1:
time: 143 us; the launch traced here: 142 us
  Pallas kernels  140 us (98%)
    pallas_call x1, Pallas kernels, reduce_to_owner(): pl.pallas_call(reduce_kernel, name='reduce', out_shape=[jax.ShapeDtypeStr...  61.4 us
    pallas_call x1, Pallas kernels, exchange_tops(): pl.pallas_call(tops_kernel, name='tops', out_shape=[jax.ShapeDtypeStruct(...  24.6 us
    pallas_call x1, Pallas kernels, clip_losses(): pl.pallas_call(loss_kernel, name='loss', out_shape=jax.ShapeDtypeStruct((...  17.2 us
    pallas_call x1, Pallas kernels, gather_kv_weight(): pl.pallas_call(kv_weight_kernel, name='kv_weight', out_shape=jax.ShapeDty...  12.5 us
    pallas_call x1, Pallas kernels, weigh(): pl.pallas_call(lambda *refs: weigh_kernel(per, *refs), name='weigh', grid...  10.6 us
    pallas_call x1, Pallas kernels, project(): pl.pallas_call(lambda *refs: project_kernel(per, *refs), name='project',...  9.31 us
    pallas_call x1, Pallas kernels, embed(): pl.pallas_call(embed_kernel, name='embed', out_shape=[jax.ShapeDtypeStruc...  3.91 us

profile of v1, /device:TPU:1, one launch (start us, length us, event | category | flops | bytes accessed | tf_op | source)
XLA Modules:
  0.0 142.1 jit_solution(4876941282346312038)
XLA Ops:
  0.6 12.5 %kv_weight.1 = bf16[2,4,128,512]{3,2,1,0:T(8,128)(2,1)} custom-call(bf16[4,128,512]{2,1,0:T(8,128)(2,1)} %bitcast.15), custom_call_target="tpu_custom_call" | custom-call | tf_op jit(solution)/shard_map/kv_weight/pallas_call | solution.py:89
  13.1 9.3 %project.1 = (bf16[16,128,512]{2,1,0:T(8,128)(2,1)}, f32[64,4,128]{2,1,0:T(4,128)}, bf16[2,128,256]{2,1,0:T(8,128)(2,1)}) custom-call(s32[16]{0:T(128)} %bitcast.19, s32[16]{0:T(128)} %refs_1_.3, s32[16]{0:T(128)} %refs_2_.3, bf16[16,128,1024]{2,1,0:T(8,128)(2,1)} %refs_3_.1, bf16[1024,512]{1,0:T(8,128)(2,1)} %bitcast.11, bf16[32,1024]{1,0:T(8,128)(2,1)} %refs_5_.1), custom_call_target="tpu_custom_call" | custom-call | tf_op jit(solution)/shard_map/project/pallas_call | solution.py:145
  22.4 24.6 %tops.1 = (f32[32,2,4,128]{3,2,1,0:T(4,128)}, f32[2,4,128]{2,1,0:T(4,128)}) custom-call(f32[32,2,4,128]{3,2,1,0:T(4,128)} %bitcast.18), custom_call_target="tpu_custom_call" | custom-call | tf_op jit(solution)/shard_map/tops/pallas_call | solution.py:225
  47.0 10.6 %weigh.1 = f32[64,264,128]{2,1,0:T(8,128)} custom-call(s32[16]{0:T(128)} %bitcast.20, s32[16]{0:T(128)} %refs_1_.3, s32[16]{0:T(128)} %refs_2_.3, bf16[16,128,512]{2,1,0:T(8,128)(2,1)} %get-tuple-element.14.refs_3_, f32[64,4,128]{2,1,0:T(4,128)} %bitcast.17, bf16[2,128,256]{2,1,0:T(8,128)(2,1)} %get-tuple-element.17.refs_5_), custom_call_target="tpu_custom_call" | custom-call | tf_op jit(solution)/shard_map/weigh/pallas_call | solution.py:279
  57.6 61.4 %reduce.3 = (f32[2,264,128]{2,1,0:T(8,128)}, bf16[2,4,128,1024]{3,2,1,0:T(8,128)(2,1)}, bf16[2,4,128,512]{3,2,1,0:T(8,128)(2,1)}) custom-call(f32[2,8,4,264,128]{4,3,2,1,0:T(8,128)} %bitcast.10, bf16[4,128,1024]{2,1,0:T(8,128)(2,1)} %bitcast.13, bf16[4,128,512]{2,1,0:T(8,128)(2,1)} %bitcast.16), custom_call_target="tpu_custom_call" | custom-call | tf_op jit(solution)/shard_map/reduce/pallas_call | solution.py:406
  119.7 3.9 %embed.1 = (bf16[2,32,1024]{2,1,0:T(8,128)(2,1)}, f32[8,128]{1,0:T(8,128)}, f32[8,128]{1,0:T(8,128)}, f32[8,128]{1,0:T(8,128)}) custom-call(s32[2]{0:T(128)} %frame.1, f32[1]{0:T(128)S(6)} %copy.14.scale, f32[2,264,128]{2,1,0:T(8,128)} %get-tuple-element.18.sums_ref, f32[2,4,128]{2,1,0:T(4,128)} %get-tuple-element.19.top_ref, bf16[32,1024]{1,0:T(8,128)(2,1)} %lat_ref.1, ...), custom_call_target="tpu_custom_call" | custom-call | tf_op jit(solution)/shard_map/embed/pallas_call | solution.py:479
  123.6 17.2 %loss.1 = f32[2,128]{1,0:T(2,128)} custom-call(f32[8,128]{1,0:T(8,128)} %get-tuple-element.23.msg_ref, f32[8,128]{1,0:T(8,128)} %get-tuple-element.24.logit_ref, f32[8,128]{1,0:T(8,128)} %get-tuple-element.25.pick_ref), custom_call_target="tpu_custom_call" | custom-call | tf_op jit(solution)/shard_map/loss/pallas_call | solution.py:573
  140.9 1.3 slice_reduce_fusion

commit v2 on v1

--- a/solution.py
+++ b/solution.py
@@ -296,10 +296,37 @@
 ORDER = (4, 3, 5, 2, 6, 1, 7, 0)
 
 
+CODE_TOP = 32767.0
+
+
+def encode(value, code_ref, meta_ref, at):
+    for kh in range(KV_HEADS):
+        part = value[kh * HEAD_DIM : (kh + 1) * HEAD_DIM]
+        largest = jnp.maximum(jnp.max(jnp.abs(part), axis=0, keepdims=True), 1e-30)
+        code = jnp.round(part * (CODE_TOP / largest)).astype(jnp.int32).astype(jnp.int16)
+        code_ref[at + (slice(kh * HEAD_DIM, (kh + 1) * HEAD_DIM), slice(None))] = code
+        meta_ref[at + (slice(4 + kh, 5 + kh), slice(None))] = largest * (1.0 / CODE_TOP)
+    meta_ref[at + (slice(0, 4), slice(None))] = value[256:260]
+
+
+def decode(code_ref, meta_ref, at):
+    parts = []
+    for kh in range(KV_HEADS):
+        code = code_ref[at + (slice(kh * HEAD_DIM, (kh + 1) * HEAD_DIM), slice(None))].astype(jnp.int32).astype(F32)
+        parts.append(code * meta_ref[at + (slice(4 + kh, 5 + kh), slice(None))])
+    return parts, meta_ref[at + (slice(0, 4), slice(None))]
+
+
+def plus(value, decoded):
+    parts, totals = decoded
+    tail = jnp.concatenate([totals, jnp.zeros((4, 128), F32)], axis=0)
+    return value + jnp.concatenate(parts + [tail], axis=0)
+
+
 def reduce_kernel(
     part_ref, wo_ref, wp_ref, out_ref, wo_out, wp_out,
-    twin_in, run, chain_in, y_in, final,
-    csend, crecv, zsend, zrecv, ysend, yrecv, wsend, wrecv, local,
+    twin_in, run, run_meta, chain_in, chain_meta, y_out, y_out_meta, y_in, y_meta,
+    csend, crecv, zsend, zrecv, msend, mrecv, ysend, yrecv, wsend, wrecv, local,
 ):
     sess, y_hi, z, core = place()
     half, _, near, far, twin = weight_peers()
@@ -335,16 +362,19 @@
         return part_ref[core, lax.rem(z + k, NZ), sub] + twin_in[k, sub]
 
     def pass_on(way, hop, sub, value):
-        run[way, hop, sub] = value
-        c = remote(
-            run.at[way, hop, sub],
-            chain_in.at[way, hop, sub],
-            zsend.at[way, hop, sub],
-            zrecv.at[way, hop, sub],
-            ways[way],
-        )
-        c.start()
-        sent[way, hop, sub] = c
+        at = (way, hop, sub)
+        encode(value, run, run_meta, at)
+        sent[at] = [
+            remote(run.at[at], chain_in.at[at], zsend.at[at], zrecv.at[at], ways[way]),
+            remote(run_meta.at[at], chain_meta.at[at], msend.at[at], mrecv.at[at], ways[way]),
+        ]
+        for c in sent[at]:
+            c.start()
+
+    def arrived(way, hop, sub):
+        for c in sent[way, hop, sub]:
+            c.wait_recv()
+        return decode(chain_in, chain_meta, (way, hop, sub))
 
     to_twin[4].wait_recv()
     for sub in range(2):
@@ -359,8 +389,7 @@
                 sub = (turn + 2) % 4 if way == 0 else turn
                 value = own_sum(ks[way], sub)
                 if (way, hop - 1, sub) in sent:
-                    sent[way, hop - 1, sub].wait_recv()
-                    value = value + chain_in[way, hop - 1, sub]
+                    value = plus(value, arrived(way, hop - 1, sub))
                 pass_on(way, hop, sub, value)
         if hop == 1:
             for first, relay in weights:
@@ -369,24 +398,35 @@
                     r.start()
 
     to_twin[0].wait_recv()
-    for sub in range(4):
+
+    def total_here(y, i):
+        sub = y * 2 + i
         value = own_sum(0, sub)
         for way in range(2):
-            sent[way, 3, sub].wait_recv()
-            value = value + chain_in[way, 3, sub]
-        final[sub] = value
+            value = plus(value, decode(chain_in, chain_meta, (way, 3, sub)))
+        return value
+
+    for sub in range(4):
+        for way in range(2):
+            for c in sent[way, 3, sub]:
+                c.wait_recv()
     over = []
     for i in range(2):
-        c = remote(final.at[(1 - y_hi) * 2 + i], y_in.at[i], ysend.at[i], yrecv.at[i], across)
-        c.start()
-        over.append(c)
+        encode(total_here(1 - y_hi, i), y_out, y_out_meta, (i,))
+        pair = [
+            remote(y_out.at[i], y_in.at[i], ysend.at[i, 0], yrecv.at[i, 0], across),
+            remote(y_out_meta.at[i], y_meta.at[i], ysend.at[i, 1], yrecv.at[i, 1], across),
+        ]
+        for c in pair:
+            c.start()
+        over.append(pair)
+    mine = [total_here(y_hi, i) for i in range(2)]
     for i in range(2):
-        over[i].wait_recv()
-        out_ref[i] = final[y_hi * 2 + i] + y_in[i]
-
-    for c in over:
-        c.wait_send()
-    for c in sent.values():
+        for c in over[i]:
+            c.wait_recv()
+        out_ref[i] = plus(mine[i], decode(y_in, y_meta, (i,)))
+
+    for c in [c for pair in over for c in pair] + [c for pair in sent.values() for c in pair]:
         c.wait_send()
     for c in to_twin.values():
         c.wait_send()
@@ -415,16 +455,22 @@
         out_specs=[VMEM_SPEC] * 3,
         scratch_shapes=[
             pltpu.VMEM((NZ, 4, SUB, 128), F32),
-            pltpu.VMEM((2, 4, 4, SUB, 128), F32),
-            pltpu.VMEM((2, 4, 4, SUB, 128), F32),
-            pltpu.VMEM((2, SUB, 128), F32),
-            pltpu.VMEM((4, SUB, 128), F32),
+            pltpu.VMEM((2, 4, 4, 256, 128), jnp.int16),
+            pltpu.VMEM((2, 4, 4, 8, 128), F32),
+            pltpu.VMEM((2, 4, 4, 256, 128), jnp.int16),
+            pltpu.VMEM((2, 4, 4, 8, 128), F32),
+            pltpu.VMEM((2, 256, 128), jnp.int16),
+            pltpu.VMEM((2, 8, 128), F32),
+            pltpu.VMEM((2, 256, 128), jnp.int16),
+            pltpu.VMEM((2, 8, 128), F32),
             dma((NZ,)),
             dma((NZ,)),
             dma((2, 4, 4)),
             dma((2, 4, 4)),
-            dma((2,)),
-            dma((2,)),
+            dma((2, 4, 4)),
+            dma((2, 4, 4)),
+            dma((2, 2)),
+            dma((2, 2)),
             dma((2, 4)),
             dma((2, 4)),
             dma((2,)),

time: 143 us -> 121 us (0.85)
  Pallas kernels: 140 us -> 118 us
    pallas_call x1, Pallas kernels: 61.4 us -> 38 us  [reduce_to_owner(): pl.pallas_call(reduce_kernel, name='reduce', out_shape=[jax.ShapeDtypeStr...]
    pallas_call x1, Pallas kernels: 17.2 us -> 18.9 us  [clip_losses(): pl.pallas_call(loss_kernel, name='loss', out_shape=jax.ShapeDtypeStruct((...]
where the time goes in v2:
time: 121 us; the launch traced here: 120 us
  Pallas kernels  118 us (98%)
  between operations  1.31 us (1%)
  local copies, waits for them, and re-layouts  1.26 us (1%)
    pallas_call x1, Pallas kernels, reduce_to_owner(): pl.pallas_call(reduce_kernel, name='reduce', out_shape=[jax.ShapeDtypeStr...  38 us
    pallas_call x1, Pallas kernels, exchange_tops(): pl.pallas_call(tops_kernel, name='tops', out_shape=[jax.ShapeDtypeStruct(...  24.6 us
    pallas_call x1, Pallas kernels, clip_losses(): pl.pallas_call(loss_kernel, name='loss', out_shape=jax.ShapeDtypeStruct((...  18.9 us
    pallas_call x1, Pallas kernels, gather_kv_weight(): pl.pallas_call(kv_weight_kernel, name='kv_weight', out_shape=jax.ShapeDty...  12.5 us
    pallas_call x1, Pallas kernels, weigh(): pl.pallas_call(lambda *refs: weigh_kernel(per, *refs), name='weigh', grid...  10.6 us
    pallas_call x1, Pallas kernels, project(): pl.pallas_call(lambda *refs: project_kernel(per, *refs), name='project',...  9.31 us
    pallas_call x1, Pallas kernels, embed(): pl.pallas_call(embed_kernel, name='embed', out_shape=[jax.ShapeDtypeStruc...  3.91 us

profile of v2, /device:TPU:1, one launch (start us, length us, event | category | flops | bytes accessed | tf_op | source)
XLA Modules:
  0.0 120.3 jit_solution(1936201776259039804)
XLA Ops:
  0.6 12.5 %kv_weight.1 = bf16[2,4,128,512]{3,2,1,0:T(8,128)(2,1)} custom-call(bf16[4,128,512]{2,1,0:T(8,128)(2,1)} %bitcast.15), custom_call_target="tpu_custom_call" | custom-call | tf_op jit(solution)/shard_map/kv_weight/pallas_call | solution.py:89
  13.1 9.3 %project.1 = (bf16[16,128,512]{2,1,0:T(8,128)(2,1)}, f32[64,4,128]{2,1,0:T(4,128)}, bf16[2,128,256]{2,1,0:T(8,128)(2,1)}) custom-call(s32[16]{0:T(128)} %bitcast.19, s32[16]{0:T(128)} %refs_1_.3, s32[16]{0:T(128)} %refs_2_.3, bf16[16,128,1024]{2,1,0:T(8,128)(2,1)} %refs_3_.1, bf16[1024,512]{1,0:T(8,128)(2,1)} %bitcast.11, bf16[32,1024]{1,0:T(8,128)(2,1)} %refs_5_.1), custom_call_target="tpu_custom_call" | custom-call | tf_op jit(solution)/shard_map/project/pallas_call | solution.py:145
  22.4 24.6 %tops.1 = (f32[32,2,4,128]{3,2,1,0:T(4,128)}, f32[2,4,128]{2,1,0:T(4,128)}) custom-call(f32[32,2,4,128]{3,2,1,0:T(4,128)} %bitcast.18), custom_call_target="tpu_custom_call" | custom-call | tf_op jit(solution)/shard_map/tops/pallas_call | solution.py:225
  47.0 10.6 %weigh.1 = f32[64,264,128]{2,1,0:T(8,128)} custom-call(s32[16]{0:T(128)} %bitcast.20, s32[16]{0:T(128)} %refs_1_.3, s32[16]{0:T(128)} %refs_2_.3, bf16[16,128,512]{2,1,0:T(8,128)(2,1)} %get-tuple-element.14.refs_3_, f32[64,4,128]{2,1,0:T(4,128)} %bitcast.17, bf16[2,128,256]{2,1,0:T(8,128)(2,1)} %get-tuple-element.17.refs_5_), custom_call_target="tpu_custom_call" | custom-call | tf_op jit(solution)/shard_map/weigh/pallas_call | solution.py:279
  57.6 38.0 %reduce.3 = (f32[2,264,128]{2,1,0:T(8,128)}, bf16[2,4,128,1024]{3,2,1,0:T(8,128)(2,1)}, bf16[2,4,128,512]{3,2,1,0:T(8,128)(2,1)}) custom-call(f32[2,8,4,264,128]{4,3,2,1,0:T(8,128)} %bitcast.10, bf16[4,128,1024]{2,1,0:T(8,128)(2,1)} %bitcast.13, bf16[4,128,512]{2,1,0:T(8,128)(2,1)} %bitcast.16), custom_call_target="tpu_custom_call" | custom-call | tf_op jit(solution)/shard_map/reduce/pallas_call | solution.py:446
  96.3 3.9 %embed.1 = (bf16[2,32,1024]{2,1,0:T(8,128)(2,1)}, f32[8,128]{1,0:T(8,128)}, f32[8,128]{1,0:T(8,128)}, f32[8,128]{1,0:T(8,128)}) custom-call(s32[2]{0:T(128)} %frame.1, f32[1]{0:T(128)S(6)} %copy.14.scale, f32[2,264,128]{2,1,0:T(8,128)} %get-tuple-element.18.sums_ref, f32[2,4,128]{2,1,0:T(4,128)} %get-tuple-element.19.top_ref, bf16[32,1024]{1,0:T(8,128)(2,1)} %lat_ref.1, ...), custom_call_target="tpu_custom_call" | custom-call | tf_op jit(solution)/shard_map/embed/pallas_call | solution.py:525
  100.2 18.9 %loss.1 = f32[2,128]{1,0:T(2,128)} custom-call(f32[8,128]{1,0:T(8,128)} %get-tuple-element.23.msg_ref, f32[8,128]{1,0:T(8,128)} %get-tuple-element.24.logit_ref, f32[8,128]{1,0:T(8,128)} %get-tuple-element.25.pick_ref), custom_call_target="tpu_custom_call" | custom-call | tf_op jit(solution)/shard_map/loss/pallas_call | solution.py:619
  119.0 1.3 %slice_reduce_fusion = f32[2]{0:T(128)} fusion(f32[2,128]{1,0:T(2,128)} %loss.1), kind=kLoop, calls=%fused_computation | loop fusion | bytes 16 | tf_op jit(solution)/shard_map/slice | solution.py:662
